TPU v7x, 512 devices: a whole 4x4x16 slice. The times are simulated.
512 devices in a mesh: blk: 128 (over y_hi, x, z), feat: 4 (over y_lo, core).
Axes of the slice: x: 4, y: 4 (y_hi: 2, y_lo: 2; y = y_hi * 2 + y_lo), z: 16, core: 2. Of those that a mesh axis runs over, the one named last changes fastest.
Arguments:
- points: bfloat16 [16384, 8192], P('blk', 'feat'), may hold values from -12 to 12
- centers: bfloat16 [2048, 8192], P('blk', 'feat'), may hold values from -12 to 12
- coefs: bfloat16 [2048, 1024], P('blk', 'feat'), may hold values from -16 to 16
Outputs:
- normal_prod: float32 [2048, 1024], P('blk', 'feat')
All inputs are finite; a program needn't handle non-finite values.
Results may differ from a plain program's by a relative error of at most 0.0011.
Values may be sent and summed in bfloat16 or wider, within the bound.
A program may use at most 64 MiB of HBM per device.

v0:
```python
import math

import jax
import jax.numpy as jnp
from jax import lax
from jax.sharding import PartitionSpec as P

F = 8192


def on_device(points, centers, coefs):
    point_sq = jnp.einsum("nf,nf->n", points, points, preferred_element_type=jnp.float32)
    center_piece = lax.all_gather(centers, "blk", axis=0, tiled=True)
    center_sq = jnp.einsum(
        "mf,mf->m", center_piece, center_piece, preferred_element_type=jnp.float32
    )
    cross_dot = lax.dot_general(
        points, center_piece, (((1,), (1,)), ((), ())), preferred_element_type=jnp.float32
    )
    dist_tile = point_sq[:, None] + center_sq[None, :] - 2.0 * cross_dot
    all_coefs = lax.all_gather(coefs, "blk", axis=0, tiled=True)
    dist = lax.psum(dist_tile, "feat")
    kernel = jnp.exp(-dist / F).astype(jnp.bfloat16)
    fitted = jnp.dot(kernel, all_coefs, preferred_element_type=jnp.float32).astype(jnp.bfloat16)
    summed = lax.psum_scatter(
        lax.dot_general(
            kernel, fitted, (((0,), (0,)), ((), ())), preferred_element_type=jnp.float32
        ),
        "blk",
        scatter_dimension=0,
        tiled=True,
    )
    point_total = points.shape[0] * lax.axis_size("blk")
    return summed * (1.0 / math.sqrt(point_total))


def solution(mesh):
    in_specs = (P("blk", "feat"), P("blk", "feat"), P("blk", "feat"))
    out_specs = P("blk", "feat")
    return jax.shard_map(
        on_device, mesh=mesh, in_specs=in_specs, out_specs=out_specs, check_vma=False
    )
```

profile of v0, /device:TPU:8, one launch (start us, length us, event | category | flops | bytes accessed | tf_op | source)
XLA Modules:
  0.0 1248.8 jit_solution(10905283807911872829)
XLA Ops:
  6.5 0.0 copy-start.1
  6.5 0.0 all-gather.3.cloned.1.call-start
  6.5 0.7 all-gather.3.cloned.1.call-update
  7.3 0.0 all-gather.5.cloned.1.call-start
  7.3 0.7 all-gather.5.cloned.1.call-update
  8.0 0.0 all-reduce.2.cloned.1.call-start
  8.1 1.2 fusion.3
  9.3 246.9 %all-gather.3.cloned.1.call-done = bf16[2048,2048]{1,0:T(8,128)(2,1)} async-done(((bf16[16,2048]{1,0:T(8,128)(2,1)}), bf16[2048,2048]{1,0:T(8,128)(2,1)}) %all-gather.3.cloned.1.call-update) | async-done | bytes 8388624 | tf_op jit(solution)/shard_map/all_gather | solution.py:13
  256.2 0.0 copy-start
  256.2 5.2 fusion
  261.5 0.0 copy-done.1
  261.5 0.5 copy-done
  262.0 3.9 fusion.1
  265.9 0.0 all-reduce.2.cloned.1.call-update
  265.9 0.0 reduce-scatter.2.cloned.1.call-start
  266.0 184.1 %all-gather.5.cloned.1.call-done = bf16[2048,256]{1,0:T(8,128)(2,1)} async-done(((bf16[16,256]{1,0:T(8,128)(2,1)}), bf16[2048,256]{1,0:T(8,128)(2,1)}) %all-gather.5.cloned.1.call-update) | async-done | bytes 1048592 | tf_op jit(solution)/shard_map/all_gather | solution.py:21
  450.1 54.6 %all-reduce.2.cloned.1.call-done = f32[128,2048]{1,0:T(8,128)} async-done(((f32[128,2048]{1,0:T(8,128)}), f32[128,2048]{1,0:T(8,128)}) %all-reduce.2.cloned.1.call-update) | async-done | bytes 1048592 | tf_op jit(solution)/shard_map/psum | solution.py:22
  504.7 4.2 fusion.2
  508.9 0.0 reduce-scatter.2.cloned.1.call-update
  508.9 732.0 %reduce-scatter.2.cloned.1.call-done = f32[16,256]{1,0:T(8,128)} async-done(((f32[2048,256]{1,0:T(8,128)}), f32[16,256]{1,0:T(8,128)}) %reduce-scatter.2.cloned.1.call-update) | async-done | bytes 16400 | tf_op jit(solution)/shard_map/reduce_scatter | solution.py:25
  1241.0 1.3 broadcast_multiply_fusion
Async XLA Ops:
  6.5 254.9 %copy-start.1 = (bf16[128,2048]{1,0:T(8,128)(2,1)S(1)}, bf16[128,2048]{1,0:T(8,128)(2,1)}, u32[]{:S(2)}) copy-start(bf16[128,2048]{1,0:T(8,128)(2,1)} %param.3) | copy-start | bytes 1572868
  6.5 249.7 %all-gather.3.cloned.1.call-start = ((), (), s32[]{:S(2)}) async-start(), calls=%async_computation.1 | async-start | bytes 8454144 | tf_op jit(solution)/shard_map/all_gather | solution.py:13
  7.3 442.8 %all-gather.5.cloned.1.call-start = ((), (), s32[]{:S(2)}) async-start(), calls=%async_computation.3 | async-start | bytes 1056768 | tf_op jit(solution)/shard_map/all_gather | solution.py:21
  8.0 496.7 %all-reduce.2.cloned.1.call-start = ((), (), s32[]{:S(2)}) async-start(), calls=%async_computation.2 | async-start | bytes 2097152 | tf_op jit(solution)/shard_map/psum | solution.py:22
  256.2 5.8 copy-start
  265.9 975.0 %reduce-scatter.2.cloned.1.call-start = ((), (), s32[]{:S(2)}) async-start(), calls=%async_computation.4 | async-start | bytes 2113536 | tf_op jit(solution)/shard_map/reduce_scatter | solution.py:25
Sparse Core Ops, SparseCore 0:
  11.8 244.3 all-gather.2
  260.5 189.5 all-gather.4
  453.1 51.5 all-reduce.1
  509.0 731.8 reduce-scatter.1
where the time goes:
time: 1250 us
  waiting for transfers between devices  1220 us (98%)
  between operations  13.1 us (1%)
    reduce_scatter x1, waiting for transfers between devices, on_device(): lax.psum_scatter(lax.dot_general(kernel, fitted, (((0,), (0,)), ((), ()))...  732 us
    all_gather x1, waiting for transfers between devices, on_device(): center_piece = lax.all_gather(centers, 'blk', axis=0, tiled=True)  247 us
    all_gather x1, waiting for transfers between devices, on_device(): all_coefs = lax.all_gather(coefs, 'blk', axis=0, tiled=True)  184 us
    psum x1, waiting for transfers between devices, on_device(): dist = lax.psum(dist_tile, 'feat')  54.6 us
  transfers between devices with their start and end apart: 4, of which 4 were waited for; matrix products, arithmetic and copies ran while one was open for 1% of the time, Pallas kernels for 0%

commit v1 on v0

v1 whole, which is shorter than its diff:
```python
import functools
import math

import jax
import jax.numpy as jnp
from jax import lax
from jax.experimental import pallas as pl
from jax.experimental.pallas import tpu as pltpu
from jax.sharding import PartitionSpec as P

MESH = pl.DeviceIdType.MESH
F32, BF16 = jnp.float32, jnp.bfloat16
NX, NY, NZ = 4, 4, 16
COPIES = 160


def kernel(
    inv_f, scale, pts, ctr, wts, out,
    px, cx, wx, dsend, dcore, dsum, r1a, r1b, r2a, r2b, kx,
    gsend, gcore, gsum, g1a, g1b, g2a, g2b, gout, zb,
    ssem, rsem, lsem,
):
    b, q = lax.axis_index("blk"), lax.axis_index("feat")
    yh, x, z = b // (NX * NZ), (b // NZ) % NX, b % NZ
    yl, c = q // 2, q % 2
    y = 2 * yh + yl
    rows, feats = pts.shape[0], pts.shape[1] // 2
    crow = ctr.shape[0]
    cblk = NZ * crow
    labels = wts.shape[1]

    def dev(yh_=None, x_=None, z_=None, q_=None):
        yh_ = yh if yh_ is None else yh_
        x_ = x if x_ is None else x_
        z_ = z if z_ is None else z_
        return ((yh_ * NX + x_) * NZ + z_, q if q_ is None else q_)

    def ydev(y_):
        return dev(yh_=y_ // 2, q_=(y_ % 2) * 2 + c)

    xp, xm, x2 = (x + 1) % NX, (x + 3) % NX, (x + 2) % NX
    yp, ym, y2 = (y + 1) % NY, (y + 3) % NY, (y + 2) % NY
    d_xp, d_xm, d_x2 = dev(x_=xp), dev(x_=xm), dev(x_=x2)
    d_zp, d_zm = dev(z_=(z + 1) % NZ), dev(z_=(z + NZ - 1) % NZ)
    d_yp, d_ym, d_y2 = ydev(yp), ydev(ym), ydev(y2)
    d_sib = dev(q_=2 * yl + 1 - c)
    d_tr = dev(x_=q, q_=x)
    diag = x == q

    used = [0]

    def new(n=1):
        used[0] += n
        assert used[0] <= COPIES
        return used[0] - n

    pending = []

    def send(i, src, dst, to):
        cp = pltpu.make_async_remote_copy(
            src_ref=src, dst_ref=dst, send_sem=ssem.at[i], recv_sem=rsem.at[i],
            device_id=to, device_id_type=MESH,
        )
        cp.start()
        pending.append(cp)

    def arrive(i, dst, frm):
        pltpu.make_async_remote_copy(
            src_ref=dst, dst_ref=dst, send_sem=ssem.at[i], recv_sem=rsem.at[i],
            device_id=frm, device_id_type=MESH,
        ).wait_recv()

    def half(ref, h):
        return ref.at[:, pl.ds(pl.multiple_of(h * feats, 128), feats)]

    def ctr_at(yh_, z_):
        return cx.at[pl.ds(pl.multiple_of(yh_ * cblk + z_ * crow, 16), crow)]

    def w_at(x_, yh_, z_):
        return wx.at[pl.ds(pl.multiple_of((2 * x_ + yh_) * cblk + z_ * crow, 16), crow)]

    def w_blk(q_, yh_, part=None):
        start, size = (2 * q_ + yh_) * cblk, cblk
        if part is not None:
            start, size = start + part * (cblk // 2), cblk // 2
        return wx.at[pl.ds(pl.multiple_of(start, 16), size)]

    loads = [
        pltpu.make_async_copy(half(ctr, yh), ctr_at(yh, z), lsem.at[0]),
        pltpu.make_async_copy(half(pts, yh), px.at[x, yh], lsem.at[1]),
    ]
    for cp in loads:
        cp.start()

    barrier = pltpu.get_barrier_semaphore()
    near = (d_zp, d_zm, d_xp, d_xm, d_x2, d_yp, d_ym, d_y2, d_sib)
    for other in near:
        pl.semaphore_signal(barrier, inc=1, device_id=other, device_id_type=MESH)

    @pl.when(jnp.logical_not(diag))
    def _():
        pl.semaphore_signal(barrier, inc=1, device_id=d_tr, device_id_type=MESH)
        pl.semaphore_wait(barrier, len(near) + 1)

    @pl.when(diag)
    def _():
        pl.semaphore_wait(barrier, len(near))

    oh = 1 - yh
    zc = [[[new() for _ in range(NZ // 2)] for _ in range(3)] for _ in range(2)]

    def z_piece(kind, zs):
        zs = (zs + NZ) % NZ
        if kind == 0:
            return ctr_at(yh, zs)
        if kind == 1:
            return ctr_at(oh, zs)
        return w_at(q, yh, zs)

    def z_last(d, kind):
        return NZ // 2 if (kind == 1) == (d == 1) else NZ // 2 - 1

    def z_send(d, kind, step, src=None):
        if step > z_last(d, kind):
            return
        sign = -1 if d == 0 else 1
        piece = z_piece(kind, z + sign * (step - 1))
        send(zc[d][kind][step - 1], piece if src is None else src, piece, d_zp if d == 0 else d_zm)

    def z_arrive(d, kind, step):
        if step > z_last(d, kind):
            return
        sign = -1 if d == 0 else 1
        arrive(zc[d][kind][step - 1], z_piece(kind, z + sign * step), d_zm if d == 0 else d_zp)

    i_sc, i_sp, i_w = new(), new(), new()
    for d in range(2):
        z_send(d, 0, 1, half(ctr, yh))
    send(i_sc, half(ctr, oh), ctr_at(yh, z), d_y2)

    @pl.when(jnp.logical_not(diag))
    def _():
        cp = pltpu.make_async_remote_copy(
            src_ref=wts, dst_ref=w_at(x, yh, z), send_sem=ssem.at[i_w], recv_sem=rsem.at[i_w],
            device_id=d_tr, device_id_type=MESH,
        )
        cp.start()

    @pl.when(diag)
    def _():
        pltpu.make_async_copy(wts, w_at(x, yh, z), lsem.at[2]).start()

    i_x = [[new(), new()] for _ in range(2)]
    i_xf = [[new(), new()] for _ in range(2)]
    hrow = rows // 2

    def x_own(j, src):
        for k, to in enumerate((d_xp, d_xm)):
            send(i_x[j][k], src, px.at[x, yh if j == 0 else oh], to)

    def x_forward(j):
        yy = yh if j == 0 else oh
        arrive(i_x[j][0], px.at[xm, yy], d_xm)
        part = px.at[xm, yy, pl.ds(0, hrow)]
        send(i_xf[j][0], part, part, d_xp)
        arrive(i_x[j][1], px.at[xp, yy], d_xp)
        part = px.at[xp, yy, pl.ds(hrow, hrow)]
        send(i_xf[j][1], part, part, d_xm)

    x_own(0, half(pts, yh))
    send(i_sp, half(pts, oh), px.at[x, yh], d_y2)

    arrive(i_sc, ctr_at(oh, z), d_y2)
    for d in range(2):
        z_send(d, 1, 1)

    @pl.when(jnp.logical_not(diag))
    def _():
        arrive(i_w, w_at(q, yh, z), d_tr)

    @pl.when(diag)
    def _():
        pltpu.make_async_copy(wts, w_at(x, yh, z), lsem.at[2]).wait()

    for d in range(2):
        z_send(d, 2, 1)

    for step in range(1, NZ // 2 + 1):
        for kind in (0, 1, 2):
            for d in range(2):
                z_arrive(d, kind, step)
                z_send(d, kind, step + 1)
        if step == 2:
            x_forward(0)
        if step == 3:
            arrive(i_sp, px.at[x, oh], d_y2)
            x_own(1, px.at[x, oh])
        if step == 5:
            x_forward(1)
    for cp in loads:
        cp.wait()

    i_wy = [new(), new()]
    i_wf = [new(), new()]
    i_ws = [new() for _ in range(5)]

    def w_y(y_, c_=c, part=None):
        return w_blk((y_ % 2) * 2 + c_, y_ // 2, part)

    send(i_wy[0], w_y(y), w_y(y), d_yp)
    send(i_wy[1], w_y(y), w_y(y), d_ym)
    send(i_ws[0], w_y(y), w_y(y), d_sib)

    cv = cx[...].astype(F32)
    csq = jnp.sum(cv * cv, axis=1, keepdims=True)
    csq = jnp.transpose(jnp.broadcast_to(csq, (csq.shape[0], 128)))[0:1, :]
    order = (x, xm, xp, x2)
    i_dc = [new() for _ in range(4)]

    def partial_dist(xs, yy):
        p = px[xs, yy]
        pf = p.astype(F32)
        psq = jnp.sum(pf * pf, axis=1, keepdims=True)
        cross = lax.dot_general(p, cx[...], (((1,), (1,)), ((), ())), preferred_element_type=F32)
        return psq + csq - 2.0 * cross

    for i, xs in enumerate(order):
        if i == 3:
            for j, yy in enumerate((yh, oh)):
                arrive(i_xf[j][0], px.at[x2, yy, pl.ds(0, hrow)], d_xm)
                arrive(i_xf[j][1], px.at[x2, yy, pl.ds(hrow, hrow)], d_xp)
        dsend[i] = partial_dist(xs, 1 - c)
        send(i_dc[i], dsend.at[i], dcore.at[i], d_sib)
        dsum[i] = partial_dist(xs, c)

    def ring(total, recv1a, recv1b, recv2a, recv2b, size, add_core, finish):
        n = len(total)
        hs = size // 2
        i1 = [[new(), new()] for _ in range(n)]
        i2 = [[new(), new()] for _ in range(n)]

        def sl(i, t, lo=0, num=size):
            return total[i](t, lo, num)

        for i in range(n):
            add_core(i)
            send(i1[i][0], sl(i, y2, 0, hs), recv1a.at[i], d_yp)
            send(i1[i][1], sl(i, y2, hs, hs), recv1b.at[i], d_ym)
        for i in range(n):
            arrive(i1[i][0], recv1a.at[i], d_ym)
            ref = sl(i, yp, 0, hs)
            ref[...] = ref[...] + recv1a[i]
            send(i2[i][0], sl(i, yp), recv2a.at[i], d_yp)
            arrive(i1[i][1], recv1b.at[i], d_yp)
            ref = sl(i, ym, hs, hs)
            ref[...] = ref[...] + recv1b[i]
            send(i2[i][1], sl(i, ym), recv2b.at[i], d_ym)
        for i in range(n):
            arrive(i2[i][0], recv2a.at[i], d_ym)
            arrive(i2[i][1], recv2b.at[i], d_yp)
            finish(i, sl(i, y)[...] + recv2a[i] + recv2b[i])

    def d_core(i):
        arrive(i_dc[i], dcore.at[i], d_sib)
        dsum[i] = dsum[i] + dcore[i]

    drow = rows // NY
    i_k = [[new() for _ in range(3)] for _ in range(4)]

    def k_at(x_, xs):
        return kx.at[x_, pl.ds(pl.multiple_of(xs * drow, 16), drow)]

    def d_finish(i, dist):
        ref = k_at(x, order[i])
        ref[...] = jnp.exp(dist * (-inv_f)).astype(BF16)
        for k, to in enumerate((d_xp, d_xm, d_x2)):
            send(i_k[i][k], ref, ref, to)

    def d_slice(i):
        return lambda t, lo, num: dsum.at[i, pl.ds(pl.multiple_of(t * drow + lo, 8), num)]

    ring([d_slice(i) for i in range(4)], r1a, r1b, r2a, r2b, drow, d_core, d_finish)

    arrive(i_wy[0], w_y(ym), d_ym)
    send(i_wf[0], w_y(ym, part=0), w_y(ym, part=0), d_yp)
    send(i_ws[1], w_y(ym), w_y(ym), d_sib)
    arrive(i_wy[1], w_y(yp), d_yp)
    send(i_wf[1], w_y(yp, part=1), w_y(yp, part=1), d_ym)
    send(i_ws[2], w_y(yp), w_y(yp), d_sib)
    arrive(i_wf[0], w_y(y2, part=0), d_ym)
    send(i_ws[3], w_y(y2, part=0), w_y(y2, part=0), d_sib)
    arrive(i_wf[1], w_y(y2, part=1), d_yp)
    send(i_ws[4], w_y(y2, part=1), w_y(y2, part=1), d_sib)
    arrive(i_ws[0], w_y(y, 1 - c), d_sib)
    arrive(i_ws[1], w_y(ym, 1 - c), d_sib)
    arrive(i_ws[2], w_y(yp, 1 - c), d_sib)
    arrive(i_ws[3], w_y(y2, 1 - c, 0), d_sib)
    arrive(i_ws[4], w_y(y2, 1 - c, 1), d_sib)

    shift = (0, 3, 1, 2)
    for i in range(4):
        for k, (xs, frm) in enumerate(((xm, d_xm), (xp, d_xp), (x2, d_x2))):
            arrive(i_k[i][k], k_at(xs, (xs + shift[i]) % NX), frm)

    fit = jnp.dot(kx[0], wx[0 : 2 * cblk], preferred_element_type=F32)
    for xs in range(1, NX):
        fit = fit + jnp.dot(
            kx[xs], wx[2 * xs * cblk : 2 * (xs + 1) * cblk], preferred_element_type=F32
        )
    fit = fit.astype(BF16)

    def contrib(y_, c_):
        kk = kx[(y_ % 2) * 2 + c_, :, pl.ds(pl.multiple_of((y_ // 2) * cblk, 128), cblk)]
        return lax.dot_general(kk, fit, (((0,), (0,)), ((), ())), preferred_element_type=F32)

    i_gc = [new() for _ in range(4)]
    gorder = (y2, yp, ym, y)
    for i, y_ in enumerate(gorder):
        gsend[i] = contrib(y_, 1 - c)
        send(i_gc[i], gsend.at[i], gcore.at[i], d_sib)
    for i, y_ in enumerate(gorder):
        gsum[y_] = contrib(y_, c)
    for i, y_ in enumerate(gorder):
        arrive(i_gc[i], gcore.at[i], d_sib)
        gsum[y_] = gsum[y_] + gcore[i]

    grow = cblk // 4
    zper = grow // crow
    i_z = new(NZ)
    zpart = [(z // zper + s) % 4 for s in (2, 1, 3, 0)]

    def g_slice(i):
        return lambda t, lo, num: gsum.at[t, pl.ds(pl.multiple_of(zpart[i] * grow + lo, 8), num)]

    def z_copy(zs, to, slot):
        return pltpu.make_async_remote_copy(
            src_ref=gout.at[pl.ds(pl.multiple_of(zs * crow, 16), crow)], dst_ref=zb.at[slot],
            send_sem=ssem.at[i_z + zs], recv_sem=rsem.at[i_z + slot],
            device_id=to, device_id_type=MESH,
        )

    def g_finish(i, val):
        gout[pl.ds(pl.multiple_of(zpart[i] * grow, 16), grow)] = val
        for j in range(zper):
            zs = zpart[i] * zper + j
            own = jnp.logical_and(diag, zs == z)

            @pl.when(jnp.logical_not(own))
            def _():
                z_copy(zs, dev(x_=q, z_=zs, q_=x), z).start()

            @pl.when(own)
            def _():
                zb[z] = val[j * crow : (j + 1) * crow]

    ring([g_slice(i) for i in range(4)], g1a, g1b, g2a, g2b, grow, lambda i: None, g_finish)

    total = None
    for s in range(NZ):
        @pl.when(jnp.logical_not(jnp.logical_and(diag, z == s)))
        def _():
            z_copy(s, dev(x_=q, z_=s, q_=x), s).wait_recv()
    for s in range(NZ):
        total = zb[s] if total is None else total + zb[s]
    out[...] = total * scale

    for cp in pending:
        cp.wait_send()

    @pl.when(jnp.logical_not(diag))
    def _():
        pltpu.make_async_remote_copy(
            src_ref=wts, dst_ref=w_at(x, yh, z), send_sem=ssem.at[i_w], recv_sem=rsem.at[i_w],
            device_id=d_tr, device_id_type=MESH,
        ).wait_send()

    for s in range(NZ):
        @pl.when(jnp.logical_not(jnp.logical_and(diag, z == s)))
        def _():
            z_copy(s, dev(x_=q, z_=s, q_=x), s).wait_send()


def solution(mesh):
    assert mesh.shape["blk"] == 2 * NX * NZ and mesh.shape["feat"] == 4

    def step(points, centers, coefs):
        rows, qf = points.shape
        crow, labels = coefs.shape
        feats, cblk = qf // 2, NZ * crow
        npts = rows * mesh.shape["blk"]
        nf = qf * mesh.shape["feat"]
        drow, grow = rows // NY, cblk // 4
        V = pltpu.VMEM
        return pl.pallas_call(
            functools.partial(kernel, 1.0 / nf, 1.0 / math.sqrt(npts)),
            out_shape=jax.ShapeDtypeStruct((crow, labels), F32),
            in_specs=[pl.BlockSpec(memory_space=pl.ANY)] * 3,
            out_specs=pl.BlockSpec(memory_space=pltpu.VMEM),
            scratch_shapes=[
                V((NX, 2, rows, feats), BF16),
                V((2 * cblk, feats), BF16),
                V((2 * NX * cblk, labels), BF16),
                V((4, rows, 2 * cblk), F32),
                V((4, rows, 2 * cblk), F32),
                V((4, rows, 2 * cblk), F32),
                V((4, drow // 2, 2 * cblk), F32),
                V((4, drow // 2, 2 * cblk), F32),
                V((4, drow, 2 * cblk), F32),
                V((4, drow, 2 * cblk), F32),
                V((NX, rows, 2 * cblk), BF16),
                V((4, cblk, labels), F32),
                V((4, cblk, labels), F32),
                V((4, cblk, labels), F32),
                V((4, grow // 2, labels), F32),
                V((4, grow // 2, labels), F32),
                V((4, grow, labels), F32),
                V((4, grow, labels), F32),
                V((cblk, labels), F32),
                V((NZ, crow, labels), F32),
                pltpu.SemaphoreType.DMA((COPIES,)),
                pltpu.SemaphoreType.DMA((COPIES,)),
                pltpu.SemaphoreType.DMA((3,)),
            ],
            compiler_params=pltpu.CompilerParams(
                collective_id=0, has_side_effects=True, vmem_limit_bytes=48 << 20
            ),
        )(points, centers, coefs)

    spec = P("blk", "feat")
    return jax.shard_map(
        step, mesh=mesh, in_specs=(spec, spec, spec), out_specs=spec, check_vma=False
    )
```

time: 1250 us -> 94.2 us (0.08)
  waiting for transfers between devices: 1220 us -> 0 us
  Pallas kernels: 0 us -> 90.8 us
  between operations: 13.1 us -> 0.01 us
    reduce_scatter x1 -> x0, waiting for transfers between devices: 732 us -> none  [on_device(): lax.psum_scatter(lax.dot_general(kernel, fitted, (((0,), (0,)), ((), ()))...]
    all_gather x2 -> x0, waiting for transfers between devices: 431 us -> none  [the longest x1 247 us: on_device(): center_piece = lax.all_gather(centers, 'blk', axis=0, tiled=True)]
    pallas_call x0 -> x1, Pallas kernels: none -> 90.8 us  [step(): pl.pallas_call(functools.partial(kernel, 1.0 / nf, 1.0 / math.sqrt(npts))...]
    psum x1 -> x0, waiting for transfers between devices: 54.6 us -> none  [on_device(): dist = lax.psum(dist_tile, 'feat')]
  transfers between devices with their start and end apart: 4 -> 0, of which waited for: 4 -> 0; matrix products, arithmetic and copies ran while one was open for 1% -> 0% of each run, Pallas kernels for 0% -> 0%
where the time goes in v1:
time: 94.2 us; the launch traced here: 94 us
  Pallas kernels  90.8 us (96%)
  local copies, waits for them, and re-layouts  3.18 us (3%)
    pallas_call x1, Pallas kernels, step(): pl.pallas_call(functools.partial(kernel, 1.0 / nf, 1.0 / math.sqrt(npts))...  90.8 us
    unnamed x7, local copies, waits for them, and re-layouts  3.18 us

profile of v1, /device:TPU:8, one launch (start us, length us, event | category | flops | bytes accessed | tf_op | source)
XLA Modules:
  0.0 94.0 jit_solution(16988605443076981246)
XLA Ops:
  0.0 0.0 copy-start
  0.0 1.0 %copy-done = bf16[128,2048]{1,0:T(8,128)(2,1)S(1)} copy-done((bf16[128,2048]{1,0:T(8,128)(2,1)S(1)}, bf16[128,2048]{1,0:T(8,128)(2,1)}, u32[]{:S(2)}) %copy-start) | copy-done | bytes 524312
  1.0 0.0 copy-start.1
  1.0 0.8 copy-done.1
  1.9 0.0 copy-start.2
  1.9 0.7 copy-done.2
  2.6 90.8 %shard_map.37 = f32[16,256]{1,0:T(8,128)S(1)} custom-call(bf16[128,2048]{1,0:T(8,128)(2,1)S(1)} %copy-done, bf16[16,2048]{1,0:T(8,128)(2,1)S(1)} %copy-done.1, bf16[16,256]{1,0:T(8,128)(2,1)S(1)} %copy-done.2), custom_call_target="tpu_custom_call" | custom-call | tf_op jit(solution)/shard_map/pallas_call | solution.py:394
  93.4 0.6 copy.5
Async XLA Ops:
  0.0 1.0 %copy-start = (bf16[128,2048]{1,0:T(8,128)(2,1)S(1)}, bf16[128,2048]{1,0:T(8,128)(2,1)}, u32[]{:S(2)}) copy-start(bf16[128,2048]{1,0:T(8,128)(2,1)} %pts.1) | copy-start | bytes 1572868
  1.0 0.8 copy-start.1
  1.9 0.7 copy-start.2

commit v2 on v0

v2 whole, which is shorter than its diff:
```python
import functools
import math

import jax
import jax.numpy as jnp
from jax import lax
from jax.experimental import pallas as pl
from jax.experimental.pallas import tpu as pltpu
from jax.sharding import PartitionSpec as P

MESH = pl.DeviceIdType.MESH
F32, BF16 = jnp.float32, jnp.bfloat16
NX, NY, NZ = 4, 4, 16
SENDS, ARRIVALS = 24, 64
REL = [0] + [s * d for d in range(1, NZ // 2) for s in (1, -1)] + [NZ // 2]
REL.remove(4), REL.insert(7, 4)
SLOT = {r: i for i, r in enumerate(REL)}
HALF = NZ // 2
OWN, LEFT, RIGHT, FAR = range(4)
UNITS = ((OWN, 0), (OWN, 1), (LEFT, 0), (RIGHT, 1), (LEFT, 1), (RIGHT, 0), (FAR, 0), (FAR, 1))
UNIT = {u: i for i, u in enumerate(UNITS)}
PIECES = ((0, 2, 0), (2, 4, 0), (4, 8, 0), (0, 4, 1), (4, 8, 1))
NEAR = [0, 1, -1, 2, -2, 3, -3, 4, -4]
NP = len(PIECES)


def kernel(
    inv_f, scale, pts, ctr, wts, out,
    px, cx, wx, kx, gsum, gout, zb, *rest,
):
    g1, g2, za, psq, fitted = rest[:5]
    dpart, dcore, r1, r2 = (rest[5 + NP * i : 5 + NP * (i + 1)] for i in range(4))
    ssem, rsem, lsem = rest[5 + 4 * NP :]
    b, q = lax.axis_index("blk"), lax.axis_index("feat")
    yh, x, z = b // (NX * NZ), (b // NZ) % NX, b % NZ
    yl, c = q // 2, q % 2
    y, oh = 2 * yh + yl, 1 - yh
    feats = pts.shape[1] // 2
    hrow = pts.shape[0] // 2
    crow = ctr.shape[0]
    cset = 2 * HALF * crow
    lab = wts.shape[1] // 2

    def dev(yh_=None, x_=None, z_=None, q_=None):
        yh_ = yh if yh_ is None else yh_
        x_ = x if x_ is None else x_
        z_ = z if z_ is None else z_
        return ((yh_ * NX + x_) * NZ + z_, q if q_ is None else q_)

    def ydev(y_):
        return dev(yh_=y_ // 2, q_=(y_ % 2) * 2 + c)

    def zat(rel):
        return (z + rel + NZ) % NZ

    xp, xm, x2 = (x + 1) % NX, (x + 3) % NX, (x + 2) % NX
    xabs = (x, xm, xp, x2)
    yp, ym, y2 = (y + 1) % NY, (y + 3) % NY, (y + 2) % NY
    d_xp, d_xm, d_x2 = dev(x_=xp), dev(x_=xm), dev(x_=x2)
    d_yp, d_ym, d_y2 = ydev(yp), ydev(ym), ydev(y2)
    d_sib = dev(q_=2 * yl + 1 - c)
    diag = x == q

    used = [0, 0]

    def counter(which, limit):
        def new():
            used[which] += 1
            assert used[which] <= limit
            return used[which] - 1
        return new

    new_s, new = counter(0, SENDS), counter(1, ARRIVALS)

    def copy(o, i, src, dst, to):
        return pltpu.make_async_remote_copy(
            src_ref=src, dst_ref=dst, send_sem=ssem.at[o], recv_sem=rsem.at[i],
            device_id=to, device_id_type=MESH,
        )

    def send(o, i, src, dst, to):
        copy(o, i, src, dst, to).start()

    def arrive(i, ref):
        copy(0, i, ref, ref, d_sib).wait_recv()

    def sent(o, ref):
        copy(o, 0, ref, ref, d_sib).wait_send()

    def half(ref, h, lo=0, num=None):
        num = ref.shape[0] if num is None else num
        return ref.at[pl.ds(lo, num), pl.ds(pl.multiple_of(h * feats, 128), feats)]

    def ctr_at(yh_, rel):
        return cx.at[SLOT[HALF if rel == -HALF else rel], yh_]

    def z_piece(kind, rel):
        if kind == 2:
            return wx.at[SLOT[HALF if rel == -HALF else rel]]
        return ctr_at(oh if kind == 1 else yh, rel)

    loads = [pltpu.make_async_copy(half(ctr, yh), z_piece(0, 0), lsem.at[0])]
    loads += [
        pltpu.make_async_copy(half(pts, yh, r * hrow, hrow), px.at[UNIT[OWN, r], yh], lsem.at[1 + r])
        for r in range(2)
    ]
    for cp in loads:
        cp.start()

    barrier = pltpu.get_barrier_semaphore()
    near = [dev(z_=zat(r)) for r in (1, -1, 2, -2)] + [d_xp, d_xm, d_x2, d_yp, d_ym, d_y2, d_sib]
    near += [dev(yh_=oh, z_=zat(r)) for r in (1, -1, 2, -2)]
    w_to = [dev(yh_=(y + n) % NY // 2, x_=q, q_=(y + n) % NY % 2 * 2 + cc) for n in range(NY) for cc in (c, 1 - c)]
    for other in near:
        pl.semaphore_signal(barrier, inc=1, device_id=other, device_id_type=MESH)
    for n, other in enumerate(w_to):
        if n:
            pl.semaphore_signal(barrier, inc=1, device_id=other, device_id_type=MESH)
    w_from = [dev(yh_=yh ^ n, x_=(q + m) % NX, q_=x) for n in range(2) for m in range(NX)]
    for n, other in enumerate(w_from):
        if n:
            pl.semaphore_signal(barrier, inc=1, device_id=other, device_id_type=MESH)

    @pl.when(jnp.logical_not(diag))
    def _():
        pl.semaphore_signal(barrier, inc=1, device_id=w_to[0], device_id_type=MESH)
        pl.semaphore_signal(barrier, inc=1, device_id=w_from[0], device_id_type=MESH)
        pl.semaphore_wait(barrier, len(near) + len(w_to) + len(w_from))

    @pl.when(diag)
    def _():
        pl.semaphore_wait(barrier, len(near) + len(w_to) + len(w_from) - 2)

    o_z, o_zw = new_s(), new_s()
    i_step = [{2: new(), 4: new(), 6: new()} for _ in range(3)]
    i_near, i_far, i_wrest = new(), new(), new()
    sign = (1, -1)

    def z_sem(kind, dist):
        if dist in i_step[kind]:
            return i_step[kind][dist]
        return i_wrest if kind == 2 else i_near if dist < 4 else i_far

    def z_there(d, kind, dist):
        return dist < HALF or (kind == 1) == (d == 1)

    def z_hop(d, kind, dist, src=None):
        for hop in (2, 1):
            if dist + hop <= HALF and z_there(d, kind, dist + hop):
                piece = z_piece(kind, -sign[d] * dist) if src is None else src
                send(o_zw if kind == 2 else o_z, z_sem(kind, dist + hop), piece,
                     z_piece(kind, -sign[d] * (dist + hop)), dev(z_=zat(sign[d] * hop)))

    def z_step(kind, dist):
        arrive(i_step[kind][dist], wx.at[0:2] if kind == 2 else cx.at[0])
        for d in range(2):
            z_hop(d, kind, dist)

    for d in range(2):
        z_hop(d, 0, 0, half(ctr, yh))
    o_sc, i_sc = new_s(), new()
    for d in range(2):
        for hop in (2, 1):
            send(o_z, z_sem(1, hop), half(ctr, oh), ctr_at(yh, -sign[d] * hop), dev(yh_=oh, z_=zat(sign[d] * hop)))
    send(o_sc, i_sc, half(ctr, oh), ctr_at(yh, 0), d_y2)

    o_x, o_sp = new_s(), new_s()
    i_sp = [new(), new()]
    i_x = [[new(), new()] for _ in range(2)]
    i_xo = [new(), new()]
    i_xf = new()
    x_to = ((d_xp, LEFT), (d_xm, RIGHT))

    def x_own(d, j, r, src=None):
        yy = oh if j else yh
        to, slot = x_to[d]
        src = px.at[UNIT[OWN, r], yy] if src is None else src
        send(o_x, i_x[d][j] if r == d else i_xo[j], src, px.at[UNIT[slot, r], yy], to)

    def x_pass(d, j):
        yy = oh if j else yh
        piece = px.at[UNIT[(LEFT, RIGHT)[d], d], yy]
        arrive(i_x[d][j], piece)
        send(o_x, i_xf, piece, px.at[UNIT[FAR, d], yy], x_to[d][0])

    for r in range(2):
        x_own(0, 0, r, half(pts, yh, r * hrow, hrow))
        x_own(1, 0, 1 - r, half(pts, yh, (1 - r) * hrow, hrow))
        send(o_sp, i_sp[r], half(pts, oh, r * hrow, hrow), px.at[UNIT[OWN, r], yh], d_y2)

    o_w, o_w0, i_w = new_s(), new_s(), new()

    def w_copy(n, local=False):
        src = wts.at[:, pl.ds(pl.multiple_of((c ^ (n % 2)) * lab, 128), lab)]
        if local:
            return pltpu.make_async_copy(src, wx.at[0, x, yh], rsem.at[i_w])
        return copy(o_w if n else o_w0, i_w, src, wx.at[0, x, yh], w_to[n])

    for n in range(1, 8):
        w_copy(n).start()

    @pl.when(jnp.logical_not(diag))
    def _():
        w_copy(0).start()

    @pl.when(diag)
    def _():
        w_copy(0, True).start()

    def square(v):
        v = v.astype(F32)
        return jnp.sum(v * v, axis=1, keepdims=True)

    csq = [None, None]

    def centers(s):
        return cx[s * HALF : (s + 1) * HALF].reshape(cset, feats)

    def set_ready(s):
        sq = square(centers(s))
        csq[s] = jnp.transpose(jnp.broadcast_to(sq, (sq.shape[0], 128)))[0:1, :]

    srow = hrow // NY
    o_dc, i_dc = new_s(), [new() for _ in range(NP)]

    def tiles(i):
        lo, hi, s = PIECES[i]
        n = (hi - lo) * 2 * hrow
        p = px[lo:hi].reshape(n, feats)
        if s == 0:
            psq[lo * 2 * hrow : hi * 2 * hrow] = square(p)
        cross = lax.dot_general(p, centers(s), (((1,), (1,)), ((), ())), preferred_element_type=F32)
        part = psq[lo * 2 * hrow : hi * 2 * hrow] + csq[s] - 2.0 * cross
        dpart[i][...] = part.reshape(hi - lo, 2, hrow, cset)
        send(o_dc, i_dc[i], dpart[i].at[:, 1 - c], dcore[i], d_sib)

    def scatter(o, total, v1, v2):
        i1, i2 = new(), new()

        def first():
            send(o, i1, total(y2, 0), v1.at[0], d_yp)
            send(o, i1, total(y2, 1), v1.at[1], d_ym)

        def second():
            arrive(i1, v1)
            for h, y_ in enumerate((yp, ym)):
                ref = total(y_, h)
                ref[...] = ref[...] + v1[h]
            send(o, i2, total(yp, None), v2.at[0], d_yp)
            send(o, i2, total(ym, None), v2.at[1], d_ym)

        def third():
            arrive(i2, v2)
            return total(y, None)[...] + v2[0] + v2[1]

        return first, second, third

    def d_slice(i):
        n = PIECES[i][1] - PIECES[i][0]

        def total(t, h):
            units = pl.ds(0, n) if h is None else pl.ds(h * (n // 2), n // 2)
            return dpart[i].at[units, c, pl.ds(pl.multiple_of(t * srow, 16), srow)]

        return total

    o_dr = new_s()
    d_ring = [scatter(o_dr, d_slice(i), r1[i], r2[i]) for i in range(NP)]

    def d_first(i):
        arrive(i_dc[i], dcore[i])
        dpart[i][:, c] = dpart[i][:, c] + dcore[i][...]
        d_ring[i][0]()

    o_k, i_k = new_s(), [new() for _ in range(4)]
    k_to = (d_xp, d_xm, d_x2, d_sib)

    def d_third(i):
        dist = d_ring[i][2]()
        val = jnp.exp(dist * (-inv_f)).astype(BF16)
        lo, hi, s = PIECES[i]
        for j in range(hi - lo):
            k, r = UNITS[lo + j]
            ref = kx.at[x, c, s, pl.ds(pl.multiple_of((xabs[k] * 2 + r) * srow, 16), srow)]
            ref[...] = val[j]
            for n, to in enumerate(k_to):
                send(o_k, i_k[n], ref, ref, to)

    z_step(0, 2)
    z_step(1, 2)
    arrive(i_sp[0], px.at[UNIT[OWN, 0], oh])
    x_own(0, 1, 0)
    x_pass(0, 0)
    x_pass(1, 0)
    z_step(0, 4)
    arrive(i_sp[1], px.at[UNIT[OWN, 1], oh])
    x_own(0, 1, 1)
    x_own(1, 1, 1)
    x_own(1, 1, 0)
    z_step(1, 4)
    for cp in loads:
        cp.wait()
    arrive(i_sc, z_piece(1, 0))
    arrive(i_near, cx.at[0:4])
    set_ready(0)
    tiles(0)
    z_step(0, 6)
    z_step(1, 6)
    arrive(i_w, wx.at[0])
    for d in range(2):
        z_hop(d, 2, 0)
    arrive(i_xo[0], px.at[0])
    x_pass(0, 1)
    x_pass(1, 1)
    d_first(0)
    tiles(1)
    d_first(1)
    d_ring[0][1]()
    arrive(i_xo[1], px.at[0])
    z_step(2, 2)
    d_ring[1][1]()
    arrive(i_xf, px.at[6:8])
    tiles(2)
    arrive(i_far, cx.at[0:5])
    set_ready(1)
    tiles(3)
    d_first(2)
    tiles(4)
    d_first(3)
    d_first(4)
    z_step(2, 4)
    d_third(0)
    d_third(1)
    d_ring[2][1]()
    d_ring[3][1]()
    d_ring[4][1]()
    z_step(2, 6)
    d_third(2)
    d_third(3)
    d_third(4)
    arrive(i_wrest, wx.at[0:9])

    for n, xs in enumerate((xm, xp, x2)):
        arrive(i_k[n], kx.at[xs, c])
        send(o_k, i_k[3], kx.at[xs, c], kx.at[xs, c], d_sib)

    def fit_of(cc):
        fit = None
        for xs in range(NX):
            for s in range(2):
                w = wx[s * HALF : (s + 1) * HALF, xs].reshape(cset, lab)
                term = jnp.dot(kx[xs, cc, s], w, preferred_element_type=F32)
                fit = term if fit is None else fit + term
        return fit.astype(BF16)

    def keep(cc):
        fitted[pl.ds(pl.multiple_of(cc * 2 * hrow, 16), 2 * hrow)] = fit_of(cc)

    keep(c)
    arrive(i_k[3], kx.at[:, 1 - c])
    keep(1 - c)

    for y_ in (y2, yp, ym, y):
        for s in range(2):
            kk = kx[y_, :, s].reshape(4 * hrow, cset)
            gsum[y_, s * cset : (s + 1) * cset] = lax.dot_general(
                kk, fitted[...], (((0,), (0,)), ((), ())), preferred_element_type=F32
            )

    grow = 2 * cset // 4
    zper = NZ // 4
    o_g, o_za, o_zn, o_z1, o_z0 = (new_s() for _ in range(5))
    i_za, i_zn, i_z0 = new(), new(), [new(), new()]
    own = jnp.logical_and(diag, y == x)

    def g_rows(rel, yy=None):
        slot = SLOT[rel]
        if yy is None:
            return gout.at[slot * 2 * crow : (slot + 1) * 2 * crow]
        return gout.at[pl.ds(pl.multiple_of((2 * slot + yy) * crow, 16), crow)]

    def z_final(rel, n):
        yy = yh ^ n
        out_sem = o_zn if rel else (o_z0, o_z1)[n]
        j = NEAR.index(rel)
        to = dev(yh_=yy, x_=y, z_=zat(rel), q_=x)
        src = g_rows(rel, yy)
        if rel:
            return copy(out_sem, i_zn, src, zb.at[c, j], to)
        return pltpu.make_async_remote_copy(
            src_ref=src, dst_ref=zb.at[c, j], send_sem=ssem.at[out_sem], recv_sem=rsem.at[i_z0[0] + c],
            device_id=to, device_id_type=MESH,
        )

    def z0_arrive(cc):
        ref = zb.at[cc, 0]
        pltpu.make_async_remote_copy(
            src_ref=ref, dst_ref=ref, send_sem=ssem.at[o_z0], recv_sem=rsem.at[i_z0[0] + cc],
            device_id=d_sib, device_id_type=MESH,
        ).wait_recv()

    def z_relay(rel):
        if rel == HALF:
            for d in range(2):
                rows = pl.ds(d * crow, crow)
                src = gout.at[pl.ds((2 * SLOT[rel] + d) * crow, crow)]
                send(o_za, i_za, src, za.at[6, rows], dev(z_=zat(4 * sign[d])))
            return
        d = 0 if rel > 0 else 1
        hop = abs(rel) - 4
        send(o_za, i_za, g_rows(rel), za.at[2 * (hop - 1) + d], dev(z_=zat(sign[d] * hop)))

    def g_slice(p):
        def total(t, h):
            lo, num = (0, grow) if h is None else (h * (grow // 2), grow // 2)
            return gsum.at[t, pl.ds(p * grow + lo, num)]

        return total

    order = (3, 2, 1, 0)
    g_ring = [scatter(o_g, g_slice(p), g1.at[p], g2.at[p]) for p in range(4)]
    for stage in range(2):
        for p in order:
            g_ring[p][stage]()
    for p in order:
        gout[p * grow : (p + 1) * grow] = g_ring[p][2]()
        for rel in reversed(REL[p * zper : (p + 1) * zper]):
            if abs(rel) > 4:
                z_relay(rel)
            elif rel and abs(rel) < 4:
                for n in range(2):
                    z_final(rel, n).start()
    z_final(0, 1).start()

    @pl.when(own)
    def _():
        zb[c, 0] = g_rows(0, yh)[...]

    arrive(i_za, za)
    for d, rel in enumerate((4, -4)):
        ref = g_rows(rel)
        ref[...] = ref[...] + za[d] + za[2 + d] + za[4 + d]
        part = gout.at[pl.ds((2 * SLOT[rel] + d) * crow, crow)]
        part[...] = part[...] + za[6, d * crow : (d + 1) * crow]
        for n in range(2):
            z_final(rel, n).start()

    @pl.when(jnp.logical_not(own))
    def _():
        z_final(0, 0).start()
        z0_arrive(c)

    z0_arrive(1 - c)
    arrive(i_zn, zb.at[:, 1:])
    for cc in range(2):
        total = zb[cc, 0]
        for j in range(1, len(NEAR)):
            total = total + zb[cc, j]
        out[:, cc * lab : (cc + 1) * lab] = total * scale

    sent(o_z, cx.at[0 : NZ - 1])
    sent(o_zw, wx.at[0 : NZ - 1])
    sent(o_sc, cx.at[0, 0])
    sent(o_x, px.at[0:6])
    sent(o_sp, px.at[0])
    sent(o_w, wx.at[0:7, 0, 0])
    sent(o_dc, cx)
    sent(o_dr, px.at[0:3])
    sent(o_k, cx.at[0:14])
    sent(o_g, px.at[0:3])
    sent(o_za, za)
    sent(o_zn, zb.at[:, 1:])
    sent(o_z1, zb.at[0, 0])

    @pl.when(jnp.logical_not(diag))
    def _():
        sent(o_w0, wx.at[0, 0, 0])

    @pl.when(jnp.logical_not(own))
    def _():
        sent(o_z0, zb.at[0, 0])


def solution(mesh):
    assert mesh.shape["blk"] == 2 * NX * NZ and mesh.shape["feat"] == 4

    def step(points, centers, coefs):
        rows, qf = points.shape
        crow, labels = coefs.shape
        feats, cset, lab = qf // 2, 2 * HALF * crow, labels // 2
        npts = rows * mesh.shape["blk"]
        nf = qf * mesh.shape["feat"]
        srow, grow, cols = rows // 2 // NY, 2 * cset // 4, cset
        V = pltpu.VMEM
        per_piece = [
            [V(shape(hi - lo), F32) for lo, hi, _ in PIECES]
            for shape in (
                lambda n: (n, 2, rows // 2, cols),
                lambda n: (n, rows // 2, cols),
                lambda n: (2, n // 2, srow, cols),
                lambda n: (2, n, srow, cols),
            )
        ]
        return pl.pallas_call(
            functools.partial(kernel, 1.0 / nf, 1.0 / math.sqrt(npts)),
            out_shape=jax.ShapeDtypeStruct((crow, labels), F32),
            in_specs=[pl.BlockSpec(memory_space=pl.ANY)] * 3,
            out_specs=pl.BlockSpec(memory_space=pltpu.VMEM),
            scratch_shapes=[
                V((2 * NX, 2, rows // 2, feats), BF16),
                V((NZ, 2, crow, feats), BF16),
                V((NZ, NX, 2, crow, lab), BF16),
                V((NX, 2, 2, rows, cset), BF16),
                V((4, 2 * cset, lab), F32),
                V((2 * cset, lab), F32),
                V((2, len(NEAR), crow, lab), F32),
                V((4, 2, grow // 2, lab), F32),
                V((4, 2, grow, lab), F32),
                V((7, 2 * crow, lab), F32),
                V((8 * rows, 1), F32),
                V((2 * rows, lab), BF16),
                *[v for group in per_piece for v in group],
                pltpu.SemaphoreType.DMA((SENDS,)),
                pltpu.SemaphoreType.DMA((ARRIVALS,)),
                pltpu.SemaphoreType.DMA((3,)),
            ],
            compiler_params=pltpu.CompilerParams(collective_id=0, has_side_effects=True),
        )(points, centers, coefs)

    spec = P("blk", "feat")
    return jax.shard_map(
        step, mesh=mesh, in_specs=(spec, spec, spec), out_specs=spec, check_vma=False
    )
```

time: 1250 us -> 78.8 us (0.06)
  the two profiles are of different devices: /device:TPU:8 before, /device:TPU:6 now
where the time goes in v2:
time: 78.8 us; the launch traced here: 78.3 us
  Pallas kernels  76.9 us (98%)
  local copies, waits for them, and re-layouts  1.32 us (2%)
    pallas_call x1, Pallas kernels, step(): pl.pallas_call(functools.partial(kernel, 1.0 / nf, 1.0 / math.sqrt(npts))...  76.9 us

profile of v2, /device:TPU:6, one launch (start us, length us, event | category | flops | bytes accessed | tf_op | source)
XLA Modules:
  0.0 78.3 jit_solution(2228091420856106411)
XLA Ops:
  0.0 76.9 %shard_map.37 = f32[16,256]{1,0:T(8,128)} custom-call(bf16[128,2048]{1,0:T(8,128)(2,1)} %pts.1, bf16[16,2048]{1,0:T(8,128)(2,1)} %ctr.1, bf16[16,256]{1,0:T(8,128)(2,1)} %wts.1), custom_call_target="tpu_custom_call" | custom-call | tf_op jit(solution)/shard_map/pallas_call | solution.py:504
  76.9 1.3 %copy.5 = f32[16,256]{1,0:T(8,128)} copy(f32[16,256]{1,0:T(8,128)} %shard_map.37) | data formatting | bytes 32768

commit v3 on v2

--- a/solution.py
+++ b/solution.py
@@ -11,7 +11,7 @@
 MESH = pl.DeviceIdType.MESH
 F32, BF16 = jnp.float32, jnp.bfloat16
 NX, NY, NZ = 4, 4, 16
-SENDS, ARRIVALS = 24, 64
+SENDS, ARRIVALS = 15, 60
 REL = [0] + [s * d for d in range(1, NZ // 2) for s in (1, -1)] + [NZ // 2]
 REL.remove(4), REL.insert(7, 4)
 SLOT = {r: i for i, r in enumerate(REL)}
@@ -30,7 +30,7 @@
 ):
     g1, g2, za, psq, fitted = rest[:5]
     dpart, dcore, r1, r2 = (rest[5 + NP * i : 5 + NP * (i + 1)] for i in range(4))
-    ssem, rsem, lsem = rest[5 + 4 * NP :]
+    ssem, rsem, lsem, hello = rest[5 + 4 * NP :]
     b, q = lax.axis_index("blk"), lax.axis_index("feat")
     yh, x, z = b // (NX * NZ), (b // NZ) % NX, b % NZ
     yl, c = q // 2, q % 2
@@ -109,59 +109,66 @@
 
     barrier = pltpu.get_barrier_semaphore()
     near = [dev(z_=zat(r)) for r in (1, -1, 2, -2)] + [d_xp, d_xm, d_x2, d_yp, d_ym, d_y2, d_sib]
-    near += [dev(yh_=oh, z_=zat(r)) for r in (1, -1, 2, -2)]
     w_to = [dev(yh_=(y + n) % NY // 2, x_=q, q_=(y + n) % NY % 2 * 2 + cc) for n in range(NY) for cc in (c, 1 - c)]
-    for other in near:
-        pl.semaphore_signal(barrier, inc=1, device_id=other, device_id_type=MESH)
-    for n, other in enumerate(w_to):
-        if n:
-            pl.semaphore_signal(barrier, inc=1, device_id=other, device_id_type=MESH)
-    w_from = [dev(yh_=yh ^ n, x_=(q + m) % NX, q_=x) for n in range(2) for m in range(NX)]
-    for n, other in enumerate(w_from):
-        if n:
-            pl.semaphore_signal(barrier, inc=1, device_id=other, device_id_type=MESH)
-
-    @pl.when(jnp.logical_not(diag))
-    def _():
-        pl.semaphore_signal(barrier, inc=1, device_id=w_to[0], device_id_type=MESH)
-        pl.semaphore_signal(barrier, inc=1, device_id=w_from[0], device_id_type=MESH)
-        pl.semaphore_wait(barrier, len(near) + len(w_to) + len(w_from))
-
-    @pl.when(diag)
-    def _():
-        pl.semaphore_wait(barrier, len(near) + len(w_to) + len(w_from) - 2)
+
+    def greet(sem, others):
+        for other in others:
+            pl.semaphore_signal(sem, inc=1, device_id=other, device_id_type=MESH)
+
+    greet(barrier, near)
+    pl.semaphore_wait(barrier, len(near))
+    greet(hello.at[0], [d_y2])
+    greet(hello.at[1], near)
 
     o_z, o_zw = new_s(), new_s()
-    i_step = [{2: new(), 4: new(), 6: new()} for _ in range(3)]
+    PARTS = 2
+    i_step = [{n: [new() for _ in range(PARTS if kind < 2 else 1)] for n in (2, 4, 6)} for kind in range(3)]
     i_near, i_far, i_wrest = new(), new(), new()
     sign = (1, -1)
 
-    def z_sem(kind, dist):
-        if dist in i_step[kind]:
-            return i_step[kind][dist]
-        return i_wrest if kind == 2 else i_near if dist < 4 else i_far
-
     def z_there(d, kind, dist):
         return dist < HALF or (kind == 1) == (d == 1)
 
-    def z_hop(d, kind, dist, src=None):
-        for hop in (2, 1):
-            if dist + hop <= HALF and z_there(d, kind, dist + hop):
-                piece = z_piece(kind, -sign[d] * dist) if src is None else src
-                send(o_zw if kind == 2 else o_z, z_sem(kind, dist + hop), piece,
-                     z_piece(kind, -sign[d] * (dist + hop)), dev(z_=zat(sign[d] * hop)))
+    def z_part(ref, part):
+        return ref.at[:, part * (feats // PARTS) : (part + 1) * (feats // PARTS)]
+
+    def z_two(d, kind, dist, part, src=None, dst=None, to=None):
+        if not z_there(d, kind, dist + 2):
+            return
+        src = z_piece(kind, -sign[d] * dist) if src is None else src
+        dst = z_piece(kind, -sign[d] * (dist + 2)) if dst is None else dst
+        to = dev(z_=zat(2 * sign[d])) if to is None else to
+        i = i_step[kind][dist + 2][part] if dist + 2 in i_step[kind] else i_wrest if kind == 2 else i_far
+        if kind == 2:
+            return send(o_zw, i, src, dst, to)
+        send(o_z, i, z_part(src, part), z_part(dst, part), to)
+
+    def z_one(d, kind, dist, src=None, dst=None, to=None):
+        src = z_piece(kind, -sign[d] * dist) if src is None else src
+        dst = z_piece(kind, -sign[d] * (dist + 1)) if dst is None else dst
+        to = dev(z_=zat(sign[d])) if to is None else to
+        i = i_wrest if kind == 2 else i_near if dist < 4 else i_far
+        send(o_zw if kind == 2 else o_z, i, src, dst, to)
+
+    def z_hop(kind, dist):
+        for part in range(len(i_step[kind][2])):
+            if dist:
+                arrive(i_step[kind][dist][part], wx.at[0:2] if kind == 2 else cx.at[0, 0])
+            for d in range(2):
+                z_two(d, kind, dist, part)
+        for d in range(2):
+            z_one(d, kind, dist)
 
     def z_step(kind, dist):
-        arrive(i_step[kind][dist], wx.at[0:2] if kind == 2 else cx.at[0])
+        z_hop(kind, dist)
+
+    mine = half(ctr, yh)
+    for part in range(PARTS):
         for d in range(2):
-            z_hop(d, kind, dist)
-
+            z_two(d, 0, 0, part, mine)
     for d in range(2):
-        z_hop(d, 0, 0, half(ctr, yh))
+        z_one(d, 0, 0, mine)
     o_sc, i_sc = new_s(), new()
-    for d in range(2):
-        for hop in (2, 1):
-            send(o_z, z_sem(1, hop), half(ctr, oh), ctr_at(yh, -sign[d] * hop), dev(yh_=oh, z_=zat(sign[d] * hop)))
     send(o_sc, i_sc, half(ctr, oh), ctr_at(yh, 0), d_y2)
 
     o_x, o_sp = new_s(), new_s()
@@ -196,16 +203,25 @@
             return pltpu.make_async_copy(src, wx.at[0, x, yh], rsem.at[i_w])
         return copy(o_w if n else o_w0, i_w, src, wx.at[0, x, yh], w_to[n])
 
-    for n in range(1, 8):
-        w_copy(n).start()
-
-    @pl.when(jnp.logical_not(diag))
-    def _():
-        w_copy(0).start()
-
-    @pl.when(diag)
-    def _():
-        w_copy(0, True).start()
+    def w_start():
+        for n in range(1, 8):
+            w_copy(n).start()
+
+        @pl.when(jnp.logical_not(diag))
+        def _():
+            w_copy(0).start()
+
+        @pl.when(diag)
+        def _():
+            w_copy(0, True).start()
+
+    pl.semaphore_wait(hello.at[0], 1)
+    other = half(ctr, oh)
+    for part in range(PARTS):
+        for d in range(2):
+            z_two(d, 1, 0, part, other, ctr_at(yh, -2 * sign[d]), dev(yh_=oh, z_=zat(2 * sign[d])))
+    for d in range(2):
+        z_one(d, 1, 0, other, ctr_at(yh, -sign[d]), dev(yh_=oh, z_=zat(sign[d])))
 
     def square(v):
         v = v.astype(F32)
@@ -287,12 +303,16 @@
                 send(o_k, i_k[n], ref, ref, to)
 
     z_step(0, 2)
+    pl.semaphore_wait(hello.at[1], len(near))
+    greet(hello.at[2], near)
+    x_pass(0, 0)
+    x_pass(1, 0)
     z_step(1, 2)
     arrive(i_sp[0], px.at[UNIT[OWN, 0], oh])
     x_own(0, 1, 0)
-    x_pass(0, 0)
-    x_pass(1, 0)
     z_step(0, 4)
+    pl.semaphore_wait(hello.at[2], len(near))
+    w_start()
     arrive(i_sp[1], px.at[UNIT[OWN, 1], oh])
     x_own(0, 1, 1)
     x_own(1, 1, 1)
@@ -305,38 +325,37 @@
     set_ready(0)
     tiles(0)
     z_step(0, 6)
-    z_step(1, 6)
-    arrive(i_w, wx.at[0])
-    for d in range(2):
-        z_hop(d, 2, 0)
-    arrive(i_xo[0], px.at[0])
     x_pass(0, 1)
     x_pass(1, 1)
+    z_step(1, 6)
+    arrive(i_xo[0], px.at[0])
     d_first(0)
     tiles(1)
+    arrive(i_w, wx.at[0])
+    z_hop(2, 0)
     d_first(1)
-    d_ring[0][1]()
-    arrive(i_xo[1], px.at[0])
-    z_step(2, 2)
-    d_ring[1][1]()
-    arrive(i_xf, px.at[6:8])
-    tiles(2)
     arrive(i_far, cx.at[0:5])
     set_ready(1)
     tiles(3)
+    d_ring[0][1]()
+    z_step(2, 2)
+    d_first(3)
+    arrive(i_xo[1], px.at[0])
+    arrive(i_xf, px.at[6:8])
+    tiles(2)
+    tiles(4)
+    d_ring[1][1]()
     d_first(2)
-    tiles(4)
-    d_first(3)
+    d_ring[3][1]()
     d_first(4)
     z_step(2, 4)
     d_third(0)
     d_third(1)
     d_ring[2][1]()
-    d_ring[3][1]()
     d_ring[4][1]()
+    d_third(3)
     z_step(2, 6)
     d_third(2)
-    d_third(3)
     d_third(4)
     arrive(i_wrest, wx.at[0:9])
 
@@ -458,6 +477,7 @@
             total = total + zb[cc, j]
         out[:, cc * lab : (cc + 1) * lab] = total * scale
 
+    assert used == [SENDS, ARRIVALS], used
     sent(o_z, cx.at[0 : NZ - 1])
     sent(o_zw, wx.at[0 : NZ - 1])
     sent(o_sc, cx.at[0, 0])
@@ -523,6 +543,7 @@
                 pltpu.SemaphoreType.DMA((SENDS,)),
                 pltpu.SemaphoreType.DMA((ARRIVALS,)),
                 pltpu.SemaphoreType.DMA((3,)),
+                pltpu.SemaphoreType.REGULAR((3,)),
             ],
             compiler_params=pltpu.CompilerParams(collective_id=0, has_side_effects=True),
         )(points, centers, coefs)

time: 78.8 us -> 76.9 us (0.976)
  Pallas kernels: 76.9 us -> 75.3 us
    pallas_call x1, Pallas kernels: 76.9 us -> 75.3 us  [step(): pl.pallas_call(functools.partial(kernel, 1.0 / nf, 1.0 / math.sqrt(npts))...]
where the time goes in v3:
time: 76.9 us; the launch traced here: 76.6 us
  Pallas kernels  75.3 us (98%)
  local copies, waits for them, and re-layouts  1.32 us (2%)
    pallas_call x1, Pallas kernels, step(): pl.pallas_call(functools.partial(kernel, 1.0 / nf, 1.0 / math.sqrt(npts))...  75.3 us

profile of v3, /device:TPU:6, one launch (start us, length us, event | category | flops | bytes accessed | tf_op | source)
XLA Modules:
  0.0 76.6 jit_solution(14163933448668038917)
XLA Ops:
  0.0 75.3 %shard_map.37 = f32[16,256]{1,0:T(8,128)} custom-call(bf16[128,2048]{1,0:T(8,128)(2,1)} %pts.1, bf16[16,2048]{1,0:T(8,128)(2,1)} %ctr.1, bf16[16,256]{1,0:T(8,128)(2,1)} %wts.1), custom_call_target="tpu_custom_call" | custom-call | tf_op jit(solution)/shard_map/pallas_call | solution.py:524
  75.3 1.3 %copy.5 = f32[16,256]{1,0:T(8,128)} copy(f32[16,256]{1,0:T(8,128)} %shard_map.37) | data formatting | bytes 32768

commit v4 on v3

--- a/solution.py
+++ b/solution.py
@@ -22,6 +22,7 @@
 PIECES = ((0, 2, 0), (2, 4, 0), (4, 8, 0), (0, 4, 1), (4, 8, 1))
 NEAR = [0, 1, -1, 2, -2, 3, -3, 4, -4]
 NP = len(PIECES)
+STOPS = ((0, 2, 4, 6, 8),) * 3
 
 
 def kernel(
@@ -117,12 +118,12 @@
 
     greet(barrier, near)
     pl.semaphore_wait(barrier, len(near))
-    greet(hello.at[0], [d_y2])
-    greet(hello.at[1], near)
+    greet(hello.at[0], near)
 
     o_z, o_zw = new_s(), new_s()
     PARTS = 2
-    i_step = [{n: [new() for _ in range(PARTS if kind < 2 else 1)] for n in (2, 4, 6)} for kind in range(3)]
+    PARTS = 2
+    i_step = [{n: [new() for _ in range(PARTS if kind < 2 else 1)] for n in STOPS[kind][1:-1]} for kind in range(3)]
     i_near, i_far, i_wrest = new(), new(), new()
     sign = (1, -1)
 
@@ -132,44 +133,35 @@
     def z_part(ref, part):
         return ref.at[:, part * (feats // PARTS) : (part + 1) * (feats // PARTS)]
 
-    def z_two(d, kind, dist, part, src=None, dst=None, to=None):
-        if not z_there(d, kind, dist + 2):
+    def z_send(d, kind, dist, hop, part=None, src=None):
+        if not z_there(d, kind, dist + hop):
             return
         src = z_piece(kind, -sign[d] * dist) if src is None else src
-        dst = z_piece(kind, -sign[d] * (dist + 2)) if dst is None else dst
-        to = dev(z_=zat(2 * sign[d])) if to is None else to
-        i = i_step[kind][dist + 2][part] if dist + 2 in i_step[kind] else i_wrest if kind == 2 else i_far
-        if kind == 2:
-            return send(o_zw, i, src, dst, to)
-        send(o_z, i, z_part(src, part), z_part(dst, part), to)
-
-    def z_one(d, kind, dist, src=None, dst=None, to=None):
-        src = z_piece(kind, -sign[d] * dist) if src is None else src
-        dst = z_piece(kind, -sign[d] * (dist + 1)) if dst is None else dst
-        to = dev(z_=zat(sign[d])) if to is None else to
-        i = i_wrest if kind == 2 else i_near if dist < 4 else i_far
-        send(o_zw if kind == 2 else o_z, i, src, dst, to)
-
-    def z_hop(kind, dist):
-        for part in range(len(i_step[kind][2])):
+        dst = z_piece(kind, -sign[d] * (dist + hop))
+        if dist + hop in i_step[kind]:
+            i = i_step[kind][dist + hop][part or 0]
+        elif kind == 2:
+            i = i_wrest
+        else:
+            i = i_near if dist + hop < 4 else i_far
+        if part is not None:
+            src, dst = z_part(src, part), z_part(dst, part)
+        send(o_zw if kind == 2 else o_z, i, src, dst, dev(z_=zat(hop * sign[d])))
+
+    def z_step(kind, dist, src=None):
+        last = STOPS[kind][STOPS[kind].index(dist) + 1] - dist
+        for part in range(PARTS if kind < 2 else 1):
             if dist:
                 arrive(i_step[kind][dist][part], wx.at[0:2] if kind == 2 else cx.at[0, 0])
             for d in range(2):
-                z_two(d, kind, dist, part)
-        for d in range(2):
-            z_one(d, kind, dist)
-
-    def z_step(kind, dist):
-        z_hop(kind, dist)
-
-    mine = half(ctr, yh)
-    for part in range(PARTS):
-        for d in range(2):
-            z_two(d, 0, 0, part, mine)
-    for d in range(2):
-        z_one(d, 0, 0, mine)
+                z_send(d, kind, dist, last, part if kind < 2 else None, src)
+        for hop in range(last - 1, 0, -1):
+            for d in range(2):
+                z_send(d, kind, dist, hop, src=src)
+
     o_sc, i_sc = new_s(), new()
     send(o_sc, i_sc, half(ctr, oh), ctr_at(yh, 0), d_y2)
+    z_step(0, 0, half(ctr, yh))
 
     o_x, o_sp = new_s(), new_s()
     i_sp = [new(), new()]
@@ -214,14 +206,6 @@
         @pl.when(diag)
         def _():
             w_copy(0, True).start()
-
-    pl.semaphore_wait(hello.at[0], 1)
-    other = half(ctr, oh)
-    for part in range(PARTS):
-        for d in range(2):
-            z_two(d, 1, 0, part, other, ctr_at(yh, -2 * sign[d]), dev(yh_=oh, z_=zat(2 * sign[d])))
-    for d in range(2):
-        z_one(d, 1, 0, other, ctr_at(yh, -sign[d]), dev(yh_=oh, z_=zat(sign[d])))
 
     def square(v):
         v = v.astype(F32)
@@ -302,62 +286,62 @@
             for n, to in enumerate(k_to):
                 send(o_k, i_k[n], ref, ref, to)
 
+    arrive(i_sc, z_piece(1, 0))
+    z_step(1, 0)
+    pl.semaphore_wait(hello.at[0], len(near))
+    greet(hello.at[1], near)
     z_step(0, 2)
-    pl.semaphore_wait(hello.at[1], len(near))
-    greet(hello.at[2], near)
     x_pass(0, 0)
     x_pass(1, 0)
-    z_step(1, 2)
+    pl.semaphore_wait(hello.at[1], len(near))
+    w_start()
     arrive(i_sp[0], px.at[UNIT[OWN, 0], oh])
     x_own(0, 1, 0)
-    z_step(0, 4)
-    pl.semaphore_wait(hello.at[2], len(near))
-    w_start()
+    z_step(1, 2)
     arrive(i_sp[1], px.at[UNIT[OWN, 1], oh])
     x_own(0, 1, 1)
     x_own(1, 1, 1)
     x_own(1, 1, 0)
-    z_step(1, 4)
+    z_step(0, 4)
     for cp in loads:
         cp.wait()
-    arrive(i_sc, z_piece(1, 0))
+    z_step(1, 4)
+    x_pass(0, 1)
+    x_pass(1, 1)
     arrive(i_near, cx.at[0:4])
     set_ready(0)
     tiles(0)
     z_step(0, 6)
-    x_pass(0, 1)
-    x_pass(1, 1)
     z_step(1, 6)
+    arrive(i_w, wx.at[0])
+    z_step(2, 0)
     arrive(i_xo[0], px.at[0])
+    tiles(1)
     d_first(0)
-    tiles(1)
-    arrive(i_w, wx.at[0])
-    z_hop(2, 0)
     d_first(1)
     arrive(i_far, cx.at[0:5])
     set_ready(1)
     tiles(3)
     d_ring[0][1]()
-    z_step(2, 2)
-    d_first(3)
     arrive(i_xo[1], px.at[0])
     arrive(i_xf, px.at[6:8])
     tiles(2)
+    d_first(3)
     tiles(4)
     d_ring[1][1]()
+    z_step(2, 2)
     d_first(2)
+    d_first(4)
     d_ring[3][1]()
-    d_first(4)
-    z_step(2, 4)
     d_third(0)
     d_third(1)
     d_ring[2][1]()
+    z_step(2, 4)
     d_ring[4][1]()
     d_third(3)
+    d_third(2)
     z_step(2, 6)
-    d_third(2)
     d_third(4)
-    arrive(i_wrest, wx.at[0:9])
 
     for n, xs in enumerate((xm, xp, x2)):
         arrive(i_k[n], kx.at[xs, c])
@@ -375,6 +359,7 @@
     def keep(cc):
         fitted[pl.ds(pl.multiple_of(cc * 2 * hrow, 16), 2 * hrow)] = fit_of(cc)
 
+    arrive(i_wrest, wx.at[0:9])
     keep(c)
     arrive(i_k[3], kx.at[:, 1 - c])
     keep(1 - c)
@@ -543,7 +528,7 @@
                 pltpu.SemaphoreType.DMA((SENDS,)),
                 pltpu.SemaphoreType.DMA((ARRIVALS,)),
                 pltpu.SemaphoreType.DMA((3,)),
-                pltpu.SemaphoreType.REGULAR((3,)),
+                pltpu.SemaphoreType.REGULAR((2,)),
             ],
             compiler_params=pltpu.CompilerParams(collective_id=0, has_side_effects=True),
         )(points, centers, coefs)

time: 76.9 us -> 75.2 us (0.978)
  Pallas kernels: 75.3 us -> 73.7 us
    pallas_call x1, Pallas kernels: 75.3 us -> 73.7 us  [step(): pl.pallas_call(functools.partial(kernel, 1.0 / nf, 1.0 / math.sqrt(npts))...]
where the time goes in v4:
time: 75.2 us; the launch traced here: 75 us
  Pallas kernels  73.7 us (98%)
  local copies, waits for them, and re-layouts  1.32 us (2%)
    pallas_call x1, Pallas kernels, step(): pl.pallas_call(functools.partial(kernel, 1.0 / nf, 1.0 / math.sqrt(npts))...  73.7 us

profile of v4, /device:TPU:6, one launch (start us, length us, event | category | flops | bytes accessed | tf_op | source)
XLA Modules:
  0.0 75.0 jit_solution(170844819296475658)
XLA Ops:
  0.0 73.7 %shard_map.37 = f32[16,256]{1,0:T(8,128)} custom-call(bf16[128,2048]{1,0:T(8,128)(2,1)} %pts.1, bf16[16,2048]{1,0:T(8,128)(2,1)} %ctr.1, bf16[16,256]{1,0:T(8,128)(2,1)} %wts.1), custom_call_target="tpu_custom_call" | custom-call | tf_op jit(solution)/shard_map/pallas_call | solution.py:509
  73.7 1.3 %copy.5 = f32[16,256]{1,0:T(8,128)} copy(f32[16,256]{1,0:T(8,128)} %shard_map.37) | data formatting | bytes 32768

commit v5 on v4

--- a/solution.py
+++ b/solution.py
@@ -11,7 +11,7 @@
 MESH = pl.DeviceIdType.MESH
 F32, BF16 = jnp.float32, jnp.bfloat16
 NX, NY, NZ = 4, 4, 16
-SENDS, ARRIVALS = 15, 60
+SENDS, ARRIVALS = 15, 63
 REL = [0] + [s * d for d in range(1, NZ // 2) for s in (1, -1)] + [NZ // 2]
 REL.remove(4), REL.insert(7, 4)
 SLOT = {r: i for i, r in enumerate(REL)}
@@ -19,7 +19,7 @@
 OWN, LEFT, RIGHT, FAR = range(4)
 UNITS = ((OWN, 0), (OWN, 1), (LEFT, 0), (RIGHT, 1), (LEFT, 1), (RIGHT, 0), (FAR, 0), (FAR, 1))
 UNIT = {u: i for i, u in enumerate(UNITS)}
-PIECES = ((0, 2, 0), (2, 4, 0), (4, 8, 0), (0, 4, 1), (4, 8, 1))
+PIECES = ((0, 2, 0), (2, 4, 0), (4, 6, 0), (6, 8, 0), (0, 4, 1), (4, 8, 1))
 NEAR = [0, 1, -1, 2, -2, 3, -3, 4, -4]
 NP = len(PIECES)
 STOPS = ((0, 2, 4, 6, 8),) * 3
@@ -283,8 +283,8 @@
             k, r = UNITS[lo + j]
             ref = kx.at[x, c, s, pl.ds(pl.multiple_of((xabs[k] * 2 + r) * srow, 16), srow)]
             ref[...] = val[j]
-            for n, to in enumerate(k_to):
-                send(o_k, i_k[n], ref, ref, to)
+            for n in (2, 0, 1, 3):
+                send(o_k, i_k[n], ref, ref, k_to[n])
 
     arrive(i_sc, z_piece(1, 0))
     z_step(1, 0)
@@ -318,30 +318,34 @@
     arrive(i_xo[0], px.at[0])
     tiles(1)
     d_first(0)
+    arrive(i_xo[1], px.at[0])
+    tiles(2)
     d_first(1)
+    d_ring[0][1]()
+    arrive(i_xf, px.at[6:8])
+    tiles(3)
+    d_first(2)
     arrive(i_far, cx.at[0:5])
     set_ready(1)
-    tiles(3)
-    d_ring[0][1]()
-    arrive(i_xo[1], px.at[0])
-    arrive(i_xf, px.at[6:8])
-    tiles(2)
+    tiles(4)
     d_first(3)
-    tiles(4)
     d_ring[1][1]()
+    tiles(5)
+    d_first(4)
+    d_ring[2][1]()
     z_step(2, 2)
-    d_first(2)
-    d_first(4)
+    d_first(5)
     d_ring[3][1]()
     d_third(0)
     d_third(1)
-    d_ring[2][1]()
+    d_third(2)
+    d_ring[4][1]()
     z_step(2, 4)
-    d_ring[4][1]()
+    d_ring[5][1]()
     d_third(3)
-    d_third(2)
+    d_third(4)
     z_step(2, 6)
-    d_third(4)
+    d_third(5)
 
     for n, xs in enumerate((xm, xp, x2)):
         arrive(i_k[n], kx.at[xs, c])
@@ -363,13 +367,6 @@
     keep(c)
     arrive(i_k[3], kx.at[:, 1 - c])
     keep(1 - c)
-
-    for y_ in (y2, yp, ym, y):
-        for s in range(2):
-            kk = kx[y_, :, s].reshape(4 * hrow, cset)
-            gsum[y_, s * cset : (s + 1) * cset] = lax.dot_general(
-                kk, fitted[...], (((0,), (0,)), ((), ())), preferred_element_type=F32
-            )
 
     grow = 2 * cset // 4
     zper = NZ // 4
@@ -423,9 +420,16 @@
 
     order = (3, 2, 1, 0)
     g_ring = [scatter(o_g, g_slice(p), g1.at[p], g2.at[p]) for p in range(4)]
-    for stage in range(2):
-        for p in order:
-            g_ring[p][stage]()
+    for s in (1, 0):
+        for y_ in (y2, yp, ym, y):
+            kk = kx[y_, :, s].reshape(4 * hrow, cset)
+            gsum[y_, s * cset : (s + 1) * cset] = lax.dot_general(
+                kk, fitted[...], (((0,), (0,)), ((), ())), preferred_element_type=F32
+            )
+        for p in order[2 - 2 * s : 4 - 2 * s]:
+            g_ring[p][0]()
+    for p in order:
+        g_ring[p][1]()
     for p in order:
         gout[p * grow : (p + 1) * grow] = g_ring[p][2]()
         for rel in reversed(REL[p * zper : (p + 1) * zper]):

time: 75.2 us -> 74.6 us (level)
  no operation moved by 1% of the time
where the time goes in v5:
time: 74.6 us; the launch traced here: 74.4 us
  Pallas kernels  73.1 us (98%)
  local copies, waits for them, and re-layouts  1.32 us (2%)
    pallas_call x1, Pallas kernels, step(): pl.pallas_call(functools.partial(kernel, 1.0 / nf, 1.0 / math.sqrt(npts))...  73.1 us

profile of v5, /device:TPU:6, one launch (start us, length us, event | category | flops | bytes accessed | tf_op | source)
XLA Modules:
  0.0 74.4 jit_solution(17453107447026624322)
XLA Ops:
  0.0 73.1 %shard_map.37 = f32[16,256]{1,0:T(8,128)} custom-call(bf16[128,2048]{1,0:T(8,128)(2,1)} %pts.1, bf16[16,2048]{1,0:T(8,128)(2,1)} %ctr.1, bf16[16,256]{1,0:T(8,128)(2,1)} %wts.1), custom_call_target="tpu_custom_call" | custom-call | tf_op jit(solution)/shard_map/pallas_call | solution.py:513
  73.1 1.3 %copy.5 = f32[16,256]{1,0:T(8,128)} copy(f32[16,256]{1,0:T(8,128)} %shard_map.37) | data formatting | bytes 32768

commit v6 on v5

--- a/solution.py
+++ b/solution.py
@@ -440,6 +440,10 @@
                     z_final(rel, n).start()
     z_final(0, 1).start()
 
+    @pl.when(jnp.logical_not(own))
+    def _():
+        z_final(0, 0).start()
+
     @pl.when(own)
     def _():
         zb[c, 0] = g_rows(0, yh)[...]
@@ -455,7 +459,6 @@
 
     @pl.when(jnp.logical_not(own))
     def _():
-        z_final(0, 0).start()
         z0_arrive(c)
 
     z0_arrive(1 - c)

time: 74.6 us -> 74.6 us (level)
  no operation moved by 1% of the time
where the time goes in v6:
time: 74.6 us; the launch traced here: 74.4 us
  Pallas kernels  73.1 us (98%)
  local copies, waits for them, and re-layouts  1.32 us (2%)
    pallas_call x1, Pallas kernels, step(): pl.pallas_call(functools.partial(kernel, 1.0 / nf, 1.0 / math.sqrt(npts))...  73.1 us

profile of v6, /device:TPU:6, one launch (start us, length us, event | category | flops | bytes accessed | tf_op | source)
XLA Modules:
  0.0 74.4 jit_solution(10464418122159584121)
XLA Ops:
  0.0 73.1 %shard_map.37 = f32[16,256]{1,0:T(8,128)} custom-call(bf16[128,2048]{1,0:T(8,128)(2,1)} %pts.1, bf16[16,2048]{1,0:T(8,128)(2,1)} %ctr.1, bf16[16,256]{1,0:T(8,128)(2,1)} %wts.1), custom_call_target="tpu_custom_call" | custom-call | tf_op jit(solution)/shard_map/pallas_call | solution.py:516
  73.1 1.3 %copy.5 = f32[16,256]{1,0:T(8,128)} copy(f32[16,256]{1,0:T(8,128)} %shard_map.37) | data formatting | bytes 32768
